TPU v7x, 32 devices: a whole 2x2x4 slice. The times are simulated.
32 devices in a mesh: patch: 8 (over z, core), visit: 4 (over y, x).
Axes of the slice: x: 2, y: 2, z: 4, core: 2. Of those that a mesh axis runs over, the one named last changes fastest.
Arguments:
- blocks: bfloat16 [8, 4, 16, 256, 256], P('patch', 'visit'), may hold values from -6 to 6
- block_patch: int32 [8, 4, 16, 1], P('patch', 'visit'), may hold values from 0 to 7; in each aligned block of 16 rows (0 to 15, 16 to 31, ..., all dimensions but the last counted through in order) at most 2 rows name the same one
- block_slot: int32 [8, 4, 16], P('patch', 'visit'), may hold values from 0 to 7
- block_count: int32 [8, 4], P('patch', 'visit'), may hold values from 12 to 16, as said below
- template: bfloat16 [8, 512, 1024], P('patch', 'visit'), may hold values from -6 to 6
- basis_rows: bfloat16 [9, 21], replicated, may hold values from -1.25 to 1.25
- basis_cols: float32 [9, 21], replicated, may hold values from -1.25 to 1.25
- coeffs: float32 [4, 9], P('visit'), may hold values from -2 to 2
- psf_rows: bfloat16 [4, 2, 25], P('visit'), may hold values from -1.25 to 1.25
- psf_cols: bfloat16 [4, 2, 25], P('visit'), may hold values from -1.25 to 1.25
Outputs:
- filtered: float32 [8, 4, 512, 1024], P('patch', 'visit')
Inputs may be any that keep to these rules, and one draw needn't show every extreme that they name: `block_patch`: among the 16 entries of one list (one patch index and visit) no patch is named more than 2 times, and some list names a patch exactly 2 times. Entries at positions block_count and beyond are unused.
All inputs are finite; a program needn't handle non-finite values.
Results may differ from a plain program's by a relative error of at most 0.005.
Values may be sent and summed in bfloat16 or wider, within the bound.
A program may use at most 128 MiB of HBM per device.

v0:
```python
import jax
import jax.numpy as jnp
from jax import lax
from jax.sharding import PartitionSpec as P

CAP = 2


def one_hot_bands(length, tile_size):
    band_shape = (3, length, tile_size, tile_size)
    side_ids = lax.broadcasted_iota(jnp.int32, band_shape, 0) - 1
    tap_ids = lax.broadcasted_iota(jnp.int32, band_shape, 1)
    inner = lax.broadcasted_iota(jnp.int32, band_shape, 2)
    outer = lax.broadcasted_iota(jnp.int32, band_shape, 3)
    return (side_ids * tile_size + inner - outer + length // 2 == tap_ids).astype(jnp.float32)


def band_tables(kernel_taps, one_hot):
    return jnp.einsum(
        "cl,dlij->cdij", kernel_taps.astype(jnp.float32), one_hot, precision=lax.Precision.HIGHEST
    ).astype(jnp.bfloat16)


def across_columns(source, tables):
    tile_size = tables.shape[-1]
    height, breadth = source.shape
    tile_count = breadth // tile_size
    tiled = source.reshape(height, tile_count, tile_size)
    zero_block = jnp.zeros((height, 1, tile_size), source.dtype)
    left_side = jnp.concatenate([zero_block, tiled[:, :-1]], axis=1)
    right_side = jnp.concatenate([tiled[:, 1:], zero_block], axis=1)
    summed = jnp.einsum("hbt,ctu->chbu", tiled, tables[:, 1], preferred_element_type=jnp.float32)
    summed = summed + jnp.einsum(
        "hbt,ctu->chbu", left_side, tables[:, 0], preferred_element_type=jnp.float32
    )
    summed = summed + jnp.einsum(
        "hbt,ctu->chbu", right_side, tables[:, 2], preferred_element_type=jnp.float32
    )
    return summed.reshape(tables.shape[0], height, breadth)


def across_rows(source, tables):
    tile_size = tables.shape[-1]
    channels, height, breadth = source.shape
    tile_count = height // tile_size
    tiled = source.reshape(channels, tile_count, tile_size, breadth)
    zero_block = jnp.zeros((channels, 1, tile_size, breadth), source.dtype)
    left_side = jnp.concatenate([zero_block, tiled[:, :-1]], axis=1)
    right_side = jnp.concatenate([tiled[:, 1:], zero_block], axis=1)
    summed = jnp.einsum("cbin,cij->bjn", tiled, tables[:, 1], preferred_element_type=jnp.float32)
    summed = summed + jnp.einsum(
        "cbin,cij->bjn", left_side, tables[:, 0], preferred_element_type=jnp.float32
    )
    summed = summed + jnp.einsum(
        "cbin,cij->bjn", right_side, tables[:, 2], preferred_element_type=jnp.float32
    )
    return summed.reshape(height, breadth)


def place_blocks(
    blocks, block_patch, block_slot, block_count, capacity, slot_total, height, breadth
):
    count_here = blocks.shape[2]
    block_edge = blocks.shape[3]
    pieces = blocks.reshape(count_here, block_edge * block_edge)
    destination = block_patch.reshape(count_here)
    slot_index = block_slot.reshape(count_here)
    row_order = lax.broadcasted_iota(jnp.int32, (count_here, count_here), 0)
    col_order = lax.broadcasted_iota(jnp.int32, (count_here, count_here), 1)
    same_patch = destination[:, None] == destination[None, :]
    earlier = jnp.sum((same_patch & (col_order < row_order)).astype(jnp.int32), axis=1)
    target = destination * capacity + earlier
    live_mask = lax.iota(jnp.int32, count_here) < block_count.reshape(())
    n_patch = lax.axis_size("patch")
    places = n_patch * capacity
    place_ids = lax.broadcasted_iota(jnp.int32, (places, count_here), 0)
    picker = ((place_ids == target[None, :]) & live_mask[None, :]).astype(jnp.float32)
    outgoing = jnp.dot(
        picker.astype(jnp.bfloat16), pieces, preferred_element_type=jnp.float32
    ).astype(jnp.bfloat16)
    outgoing = outgoing.reshape(n_patch, capacity, block_edge * block_edge)
    labels = (
        jnp.dot(
            picker, (slot_index - slot_total).astype(jnp.float32), precision=lax.Precision.HIGHEST
        )
        + slot_total
    )
    labels = labels.astype(jnp.bfloat16).reshape(n_patch, capacity)
    arrived, arrived_slots = (
        lax.all_to_all(outgoing, "patch", split_axis=0, concat_axis=0, tiled=True),
        lax.all_to_all(labels, "patch", split_axis=0, concat_axis=0, tiled=True),
    )
    arrived = arrived.reshape(places, block_edge * block_edge)
    slot_ids = lax.broadcasted_iota(jnp.float32, (slot_total, places), 0)
    chosen = (slot_ids == arrived_slots.reshape(1, places).astype(jnp.float32)).astype(jnp.bfloat16)
    placed = jnp.dot(chosen, arrived, preferred_element_type=jnp.float32)
    tall_count = height // block_edge
    wide_count = breadth // block_edge
    placed = placed.reshape(tall_count, wide_count, block_edge, block_edge).transpose(0, 2, 1, 3)
    return placed.reshape(height, breadth)


def per_device(
    blocks,
    block_patch,
    block_slot,
    block_count,
    template,
    basis_rows,
    basis_cols,
    coeffs,
    psf_rows,
    psf_cols,
):
    local_rows = template.shape[1]
    breadth = template.shape[2]
    height = local_rows * lax.axis_size("visit")
    block_edge = blocks.shape[3]
    slot_total = height // block_edge * (breadth // block_edge)
    science = place_blocks(
        blocks, block_patch, block_slot, block_count, CAP, slot_total, height, breadth
    )
    column_hot = one_hot_bands(basis_rows.shape[1], min(128, breadth))
    row_hot = one_hot_bands(basis_cols.shape[1], min(128, height))
    scaled = (coeffs[0][:, None] * basis_cols).astype(jnp.bfloat16)
    start_image = jnp.zeros((height, breadth), jnp.float32)
    all_tables = band_tables(basis_rows, column_hot)
    partial_rows = across_columns(template[0], all_tables).astype(jnp.bfloat16)
    smoothed_all = lax.all_gather(partial_rows, "visit", axis=1, tiled=True)

    def per_stack(model_image, profiles):
        smoothed, col_taps = profiles
        col_table = band_tables(col_taps[None], row_hot)
        return (model_image + across_rows(smoothed[None], col_table), None)

    model_image = lax.scan(per_stack, start_image, (smoothed_all, scaled))[0]
    difference = (science - model_image).astype(jnp.bfloat16)
    psf_column_hot = one_hot_bands(psf_rows.shape[2], min(128, breadth))
    psf_row_hot = one_hot_bands(psf_cols.shape[2], min(128, height))
    blurred = across_columns(difference, band_tables(psf_rows[0], psf_column_hot)).astype(
        jnp.bfloat16
    )
    filtered = across_rows(blurred, band_tables(psf_cols[0], psf_row_hot))
    return filtered[None, None]


def solution(mesh):
    placed = (
        P("patch", "visit", None, None, None),
        P("patch", "visit", None, None),
        P("patch", "visit", None),
        P("patch", "visit"),
        P("patch", "visit", None),
        P(),
        P(),
        P("visit", None),
        P("visit", None, None),
        P("visit", None, None),
    )
    return jax.shard_map(
        per_device,
        mesh=mesh,
        in_specs=placed,
        out_specs=P("patch", "visit", None, None),
        check_vma=False,
    )
```

profile of v0, /device:TPU:0, one launch (start us, length us, event | category | flops | bytes accessed | tf_op | source)
XLA Modules:
  0.0 238.5 jit_solution(14624126274584516626)
XLA Ops:
  16.9 6.4 %all-to-all-start = ((bf16[8,1,2]{2,1,0:T(2,128)(2,1)}), bf16[8,1,2]{2,1,0:T(2,128)(2,1)S(1)}, u32[]{:S(2)}, u32[]{:S(2)}) async-start(bf16[8,1,2]{2,1,0:T(2,128)(2,1)} %all_to_all.12), calls=%async_computation | async-start | bytes 8192 | tf_op jit(solution)/shard_map/all_to_all | solution.py:91
  28.8 4.5 %all-to-all-start.1 = ((bf16[8,2,65536]{2,1,0:T(2,128)(2,1)}), bf16[8,2,65536]{2,1,0:T(2,128)(2,1)}, u32[]{:S(2)}, u32[]{:S(2)}) async-start(bf16[8,2,65536]{2,1,0:T(2,128)(2,1)} %reshape.116), calls=%async_computation.1 | async-start | bytes 4194304 | tf_op jit(solution)/shard_map/all_to_all | solution.py:90
  37.3 44.9 %all-to-all-done.1 = bf16[8,2,65536]{2,1,0:T(2,128)(2,1)} async-done(((bf16[8,2,65536]{2,1,0:T(2,128)(2,1)}), bf16[8,2,65536]{2,1,0:T(2,128)(2,1)}, u32[]{:S(2)}, u32[]{:S(2)}) %all-to-all-start.1) | async-done | bytes 2097184 | tf_op jit(solution)/shard_map/all_to_all | solution.py:90
  87.1 27.0 %all-gather.2.cloned.1.call-done = bf16[9,512,1024]{2,1,0:T(8,128)(2,1)} async-done(((bf16[9,128,1024]{2,1,0:T(8,128)(2,1)}), bf16[9,512,1024]{2,1,0:T(8,128)(2,1)}) %all-gather.2.cloned.1.call-update) | async-done | bytes 9437200 | tf_op jit(solution)/shard_map/all_gather | solution.py:129
  114.1 97.7 %while.11 = (s32[]{:T(128)}, f32[512,1024]{1,0:T(8,128)}, bf16[9,21]{1,0:T(8,128)(2,1)S(1)}, bf16[9,512,1024]{2,1,0:T(8,128)(2,1)}, s32[3]{0:T(128)S(1)}, /*index=5*/s32[]{:T(128)}, s32[]{:T(128)}) while((s32[]{:T(128)}, f32[512,1024]{1,0:T(8,128)}, bf16[9,21]{1,0:T(8,128)(2,1)S(1)}, bf16[9,512,1024]{2,1,0:T(8,128)(2,1)}, ...), condition=%wide.region_2.3_spmd.clone, body=%wide.region_1.2_spmd.clone.sunk | while | flops 422297600 | bytes 33489512 | solution.py:136
  114.7 4.0 %fusion.117 = bf16[1,3,128,128]{3,0,2,1:T(2,128)(2,1)S(1)} fusion(f32[3,21,128,128]{3,2,1,0:T(8,128)S(1)} %fusion.116, bf16[9,21]{1,0:T(8,128)(2,1)S(1)} %get-tuple-element.132, s32[]{:T(128)} %get-tuple-element.123), kind=kOutput, calls=%fused_computation.1.clone.1 | convolution fusion | flops 12386304 | bytes 4227588 | tf_op jit(solution)/shard_map/while/body/eval_jaxpr/cl,dlij->cdij/dot_general | solution.py:19
  124.1 4.0 %fusion.117 = bf16[1,3,128,128]{3,0,2,1:T(2,128)(2,1)S(1)} fusion(f32[3,21,128,128]{3,2,1,0:T(8,128)S(1)} %fusion.116, bf16[9,21]{1,0:T(8,128)(2,1)S(1)} %get-tuple-element.132, s32[]{:T(128)} %get-tuple-element.123), kind=kOutput, calls=%fused_computation.1.clone.1 | convolution fusion | flops 12386304 | bytes 4227588 | tf_op jit(solution)/shard_map/while/body/eval_jaxpr/cl,dlij->cdij/dot_general | solution.py:19
  131.0 3.6 %bitcast_add_fusion.4 = f32[512,1024]{1,0:T(8,128)} fusion(f32[128,4,1024]{2,0,1:T(8,128)S(1)} %add_add_fusion.2, f32[512,1024]{1,0:T(8,128)} %get-tuple-element.124, pred[]{:T(512)S(6)} %compare.11), kind=kLoop, calls=%fused_computation.5.clone.1 | loop fusion | flops 1048576 | bytes 6291457 | tf_op jit(solution)/shard_map/while/body/eval_jaxpr/add | solution.py:134
  135.2 4.0 %fusion.117 = bf16[1,3,128,128]{3,0,2,1:T(2,128)(2,1)S(1)} fusion(f32[3,21,128,128]{3,2,1,0:T(8,128)S(1)} %fusion.116, bf16[9,21]{1,0:T(8,128)(2,1)S(1)} %get-tuple-element.132, s32[]{:T(128)} %get-tuple-element.123), kind=kOutput, calls=%fused_computation.1.clone.1 | convolution fusion | flops 12386304 | bytes 4227588 | tf_op jit(solution)/shard_map/while/body/eval_jaxpr/cl,dlij->cdij/dot_general | solution.py:19
  142.0 3.6 %bitcast_add_fusion.4 = f32[512,1024]{1,0:T(8,128)} fusion(f32[128,4,1024]{2,0,1:T(8,128)S(1)} %add_add_fusion.2, f32[512,1024]{1,0:T(8,128)} %get-tuple-element.124, pred[]{:T(512)S(6)} %compare.11), kind=kLoop, calls=%fused_computation.5.clone.1 | loop fusion | flops 1048576 | bytes 6291457 | tf_op jit(solution)/shard_map/while/body/eval_jaxpr/add | solution.py:134
  146.2 4.0 %fusion.117 = bf16[1,3,128,128]{3,0,2,1:T(2,128)(2,1)S(1)} fusion(f32[3,21,128,128]{3,2,1,0:T(8,128)S(1)} %fusion.116, bf16[9,21]{1,0:T(8,128)(2,1)S(1)} %get-tuple-element.132, s32[]{:T(128)} %get-tuple-element.123), kind=kOutput, calls=%fused_computation.1.clone.1 | convolution fusion | flops 12386304 | bytes 4227588 | tf_op jit(solution)/shard_map/while/body/eval_jaxpr/cl,dlij->cdij/dot_general | solution.py:19
  153.1 3.6 %bitcast_add_fusion.4 = f32[512,1024]{1,0:T(8,128)} fusion(f32[128,4,1024]{2,0,1:T(8,128)S(1)} %add_add_fusion.2, f32[512,1024]{1,0:T(8,128)} %get-tuple-element.124, pred[]{:T(512)S(6)} %compare.11), kind=kLoop, calls=%fused_computation.5.clone.1 | loop fusion | flops 1048576 | bytes 6291457 | tf_op jit(solution)/shard_map/while/body/eval_jaxpr/add | solution.py:134
  157.2 4.0 %fusion.117 = bf16[1,3,128,128]{3,0,2,1:T(2,128)(2,1)S(1)} fusion(f32[3,21,128,128]{3,2,1,0:T(8,128)S(1)} %fusion.116, bf16[9,21]{1,0:T(8,128)(2,1)S(1)} %get-tuple-element.132, s32[]{:T(128)} %get-tuple-element.123), kind=kOutput, calls=%fused_computation.1.clone.1 | convolution fusion | flops 12386304 | bytes 4227588 | tf_op jit(solution)/shard_map/while/body/eval_jaxpr/cl,dlij->cdij/dot_general | solution.py:19
  164.1 3.6 %bitcast_add_fusion.4 = f32[512,1024]{1,0:T(8,128)} fusion(f32[128,4,1024]{2,0,1:T(8,128)S(1)} %add_add_fusion.2, f32[512,1024]{1,0:T(8,128)} %get-tuple-element.124, pred[]{:T(512)S(6)} %compare.11), kind=kLoop, calls=%fused_computation.5.clone.1 | loop fusion | flops 1048576 | bytes 6291457 | tf_op jit(solution)/shard_map/while/body/eval_jaxpr/add | solution.py:134
  168.3 4.0 %fusion.117 = bf16[1,3,128,128]{3,0,2,1:T(2,128)(2,1)S(1)} fusion(f32[3,21,128,128]{3,2,1,0:T(8,128)S(1)} %fusion.116, bf16[9,21]{1,0:T(8,128)(2,1)S(1)} %get-tuple-element.132, s32[]{:T(128)} %get-tuple-element.123), kind=kOutput, calls=%fused_computation.1.clone.1 | convolution fusion | flops 12386304 | bytes 4227588 | tf_op jit(solution)/shard_map/while/body/eval_jaxpr/cl,dlij->cdij/dot_general | solution.py:19
  175.1 3.6 %bitcast_add_fusion.4 = f32[512,1024]{1,0:T(8,128)} fusion(f32[128,4,1024]{2,0,1:T(8,128)S(1)} %add_add_fusion.2, f32[512,1024]{1,0:T(8,128)} %get-tuple-element.124, pred[]{:T(512)S(6)} %compare.11), kind=kLoop, calls=%fused_computation.5.clone.1 | loop fusion | flops 1048576 | bytes 6291457 | tf_op jit(solution)/shard_map/while/body/eval_jaxpr/add | solution.py:134
  179.3 4.0 %fusion.117 = bf16[1,3,128,128]{3,0,2,1:T(2,128)(2,1)S(1)} fusion(f32[3,21,128,128]{3,2,1,0:T(8,128)S(1)} %fusion.116, bf16[9,21]{1,0:T(8,128)(2,1)S(1)} %get-tuple-element.132, s32[]{:T(128)} %get-tuple-element.123), kind=kOutput, calls=%fused_computation.1.clone.1 | convolution fusion | flops 12386304 | bytes 4227588 | tf_op jit(solution)/shard_map/while/body/eval_jaxpr/cl,dlij->cdij/dot_general | solution.py:19
  186.2 3.6 %bitcast_add_fusion.4 = f32[512,1024]{1,0:T(8,128)} fusion(f32[128,4,1024]{2,0,1:T(8,128)S(1)} %add_add_fusion.2, f32[512,1024]{1,0:T(8,128)} %get-tuple-element.124, pred[]{:T(512)S(6)} %compare.11), kind=kLoop, calls=%fused_computation.5.clone.1 | loop fusion | flops 1048576 | bytes 6291457 | tf_op jit(solution)/shard_map/while/body/eval_jaxpr/add | solution.py:134
  190.3 4.0 %fusion.117 = bf16[1,3,128,128]{3,0,2,1:T(2,128)(2,1)S(1)} fusion(f32[3,21,128,128]{3,2,1,0:T(8,128)S(1)} %fusion.116, bf16[9,21]{1,0:T(8,128)(2,1)S(1)} %get-tuple-element.132, s32[]{:T(128)} %get-tuple-element.123), kind=kOutput, calls=%fused_computation.1.clone.1 | convolution fusion | flops 12386304 | bytes 4227588 | tf_op jit(solution)/shard_map/while/body/eval_jaxpr/cl,dlij->cdij/dot_general | solution.py:19
  197.2 3.6 %bitcast_add_fusion.4 = f32[512,1024]{1,0:T(8,128)} fusion(f32[128,4,1024]{2,0,1:T(8,128)S(1)} %add_add_fusion.2, f32[512,1024]{1,0:T(8,128)} %get-tuple-element.124, pred[]{:T(512)S(6)} %compare.11), kind=kLoop, calls=%fused_computation.5.clone.1 | loop fusion | flops 1048576 | bytes 6291457 | tf_op jit(solution)/shard_map/while/body/eval_jaxpr/add | solution.py:134
  201.4 4.0 %fusion.117 = bf16[1,3,128,128]{3,0,2,1:T(2,128)(2,1)S(1)} fusion(f32[3,21,128,128]{3,2,1,0:T(8,128)S(1)} %fusion.116, bf16[9,21]{1,0:T(8,128)(2,1)S(1)} %get-tuple-element.132, s32[]{:T(128)} %get-tuple-element.123), kind=kOutput, calls=%fused_computation.1.clone.1 | convolution fusion | flops 12386304 | bytes 4227588 | tf_op jit(solution)/shard_map/while/body/eval_jaxpr/cl,dlij->cdij/dot_general | solution.py:19
  208.2 3.6 %bitcast_add_fusion.4 = f32[512,1024]{1,0:T(8,128)} fusion(f32[128,4,1024]{2,0,1:T(8,128)S(1)} %add_add_fusion.2, f32[512,1024]{1,0:T(8,128)} %get-tuple-element.124, pred[]{:T(512)S(6)} %compare.11), kind=kLoop, calls=%fused_computation.5.clone.1 | loop fusion | flops 1048576 | bytes 6291457 | tf_op jit(solution)/shard_map/while/body/eval_jaxpr/add | solution.py:134
  211.8 3.0 %copy.82 = f32[512,1024]{0,1:T(8,128)} copy(f32[512,1024]{1,0:T(8,128)} %get-tuple-element.32) | data formatting | bytes 4194304 | tf_op jit(solution)/shard_map/while | solution.py:136
  225.5 3.0 %copy.90 = bf16[2,4,128,1024]{3,2,0,1:T(8,128)(2,1)S(1)} copy(bf16[2,4,128,1024]{2,1,3,0:T(4,128)(2,1)} %convert_element_type.117) | data formatting | bytes 4194304 | tf_op jit(solution)/shard_map/convert_element_type | solution.py:140
  (147 shorter events, 70.6 us)
Async XLA Ops:
  6.5 0.7 copy-start
  6.5 107.6 %all-gather.2.cloned.1.call-start = ((), (), s32[]{:S(2)}) async-start(), calls=%async_computation.2 | async-start | bytes 11796480 | tf_op jit(solution)/shard_map/all_gather | solution.py:129
  8.6 1.0 copy-start.5
  15.0 0.8 copy-start.8
  15.0 1.0 copy-start.9
  15.0 8.2 %copy-start.4 = (bf16[1,1,16,256,256]{4,3,2,1,0:T(8,128)(2,1)S(1)}, bf16[1,1,16,256,256]{4,3,2,1,0:T(8,128)(2,1)}, u32[]{:S(2)}) copy-start(bf16[1,1,16,256,256]{4,3,2,1,0:T(8,128)(2,1)} %param.12) | copy-start | bytes 6291460
  16.9 11.9 %all-to-all-start = ((bf16[8,1,2]{2,1,0:T(2,128)(2,1)}), bf16[8,1,2]{2,1,0:T(2,128)(2,1)S(1)}, u32[]{:S(2)}, u32[]{:S(2)}) async-start(bf16[8,1,2]{2,1,0:T(2,128)(2,1)} %all_to_all.12), calls=%async_computation | async-start | bytes 8192 | tf_op jit(solution)/shard_map/all_to_all | solution.py:91
  27.4 5.9 %copy-start.10 = (bf16[1,2,25]{2,1,0:T(2,128)(2,1)S(1)}, bf16[1,2,25]{2,1,0:T(2,128)(2,1)}, u32[]{:S(2)}) copy-start(bf16[1,2,25]{2,1,0:T(2,128)(2,1)} %param.21) | copy-start | bytes 304
  28.8 53.4 %all-to-all-start.1 = ((bf16[8,2,65536]{2,1,0:T(2,128)(2,1)}), bf16[8,2,65536]{2,1,0:T(2,128)(2,1)}, u32[]{:S(2)}, u32[]{:S(2)}) async-start(bf16[8,2,65536]{2,1,0:T(2,128)(2,1)} %reshape.116), calls=%async_computation.1 | async-start | bytes 4194304 | tf_op jit(solution)/shard_map/all_to_all | solution.py:90
  33.3 2.1 copy-start.6
  33.4 2.1 copy-start.7
  33.4 2.1 copy-start.11
  211.8 3.0 %copy-start.2 = (f32[512,1024]{0,1:T(8,128)S(1)}, f32[512,1024]{0,1:T(8,128)}, u32[]{:S(2)}) copy-start(f32[512,1024]{0,1:T(8,128)} %copy.81) | copy-start | bytes 6291460
  221.5 1.2 copy-start.3
  229.8 1.9 copy-start.1
Sparse Core Ops, SparseCore 0:
  15.1 98.9 all-gather.1
where the time goes:
time: 240 us; the launch traced here: 239 us
  waiting for transfers between devices  73.3 us (31%)
  matrix products  59.7 us (25%)
  local copies, waits for them, and re-layouts  41.5 us (17%)
  other arithmetic  38.2 us (16%)
  between operations  14.5 us (6%)
  starting transfers between devices  10.9 us (5%)
    all_to_all x1, waiting for transfers between devices, place_blocks(): lax.all_to_all(outgoing, 'patch', split_axis=0, concat_axis=0, tiled=True)  44.9 us
    dot_general x12, matrix products, band_tables(): jnp.einsum('cl,dlij->cdij', kernel_taps.astype(jnp.float32), one_hot, pre...  39.9 us
    add x9, other arithmetic, per_stack(): return (model_image + across_rows(smoothed[None], col_table), None)  30.6 us
    all_gather x1, waiting for transfers between devices, per_device(): smoothed_all = lax.all_gather(partial_rows, 'visit', axis=1, tiled=True)  27 us
    dynamic_slice x9, local copies, waits for them, and re-layouts, per_device(): model_image = lax.scan(per_stack, start_image, (smoothed_all, scaled))[0]  11.7 us
    unnamed x31, local copies, waits for them, and re-layouts  6.85 us
    all_to_all x1, starting transfers between devices, place_blocks(): lax.all_to_all(labels, 'patch', split_axis=0, concat_axis=0, tiled=True)  6.35 us
    dot_general x10, matrix products, across_rows(): jnp.einsum('cbin,cij->bjn', left_side, tables[:, 0], preferred_element_ty...  5.32 us
  transfers between devices with their start and end apart: 3, of which 3 were waited for; matrix products, arithmetic and copies ran while one was open for 6% of the time, Pallas kernels for 0%

commit v1 on v0

--- a/solution.py
+++ b/solution.py
@@ -1,9 +1,18 @@
+import functools
 import jax
 import jax.numpy as jnp
 from jax import lax
 from jax.sharding import PartitionSpec as P
 
 CAP = 2
+
+
+def _bind_sheets(here_x, ndim_at):
+    low = jnp.concatenate(lax.all_gather(here_x, "visit"), ndim_at)
+    return low
+
+
+pass_leaf = functools.partial(_bind_sheets, ndim_at=1)
 
 
 def one_hot_bands(length, tile_size):
@@ -126,7 +135,7 @@
     start_image = jnp.zeros((height, breadth), jnp.float32)
     all_tables = band_tables(basis_rows, column_hot)
     partial_rows = across_columns(template[0], all_tables).astype(jnp.bfloat16)
-    smoothed_all = lax.all_gather(partial_rows, "visit", axis=1, tiled=True)
+    smoothed_all = pass_leaf(partial_rows)
 
     def per_stack(model_image, profiles):
         smoothed, col_taps = profiles

time: 240 us -> 248 us (1.033)
  local copies, waits for them, and re-layouts: 41.5 us -> 50.7 us
    all_gather x0 -> x1, local copies, waits for them, and re-layouts: none -> 9.22 us  [_bind_sheets(): low = jnp.concatenate(lax.all_gather(here_x, 'visit'), ndim_at)]
  transfers between devices with their start and end apart: 3 -> 3, of which waited for: 3 -> 3; matrix products, arithmetic and copies ran while one was open for 6% -> 5% of each run, Pallas kernels for 0% -> 0%
where the time goes in v1:
time: 248 us; the launch traced here: 247 us
  waiting for transfers between devices  73.2 us (30%)
  matrix products  59.7 us (24%)
  local copies, waits for them, and re-layouts  50.7 us (20%)
  other arithmetic  37.4 us (15%)
  between operations  14.5 us (6%)
  starting transfers between devices  10.9 us (4%)
    all_to_all x1, waiting for transfers between devices, place_blocks(): lax.all_to_all(outgoing, 'patch', split_axis=0, concat_axis=0, tiled=True)  44.9 us
    dot_general x12, matrix products, band_tables(): jnp.einsum('cl,dlij->cdij', kernel_taps.astype(jnp.float32), one_hot, pre...  39.9 us
    add x9, other arithmetic, per_stack(): return (model_image + across_rows(smoothed[None], col_table), None)  29.8 us
    all_gather x1, waiting for transfers between devices, _bind_sheets(): low = jnp.concatenate(lax.all_gather(here_x, 'visit'), ndim_at)  26.9 us
    dynamic_slice x9, local copies, waits for them, and re-layouts, per_device(): model_image = lax.scan(per_stack, start_image, (smoothed_all, scaled))[0]  11.7 us
    all_gather x1, local copies, waits for them, and re-layouts, _bind_sheets(): low = jnp.concatenate(lax.all_gather(here_x, 'visit'), ndim_at)  9.22 us
    unnamed x31, local copies, waits for them, and re-layouts  6.84 us
    all_to_all x1, starting transfers between devices, place_blocks(): lax.all_to_all(labels, 'patch', split_axis=0, concat_axis=0, tiled=True)  6.35 us
  transfers between devices with their start and end apart: 3, of which 3 were waited for; matrix products, arithmetic and copies ran while one was open for 5% of the time, Pallas kernels for 0%

profile of v1, /device:TPU:0, one launch (start us, length us, event | category | flops | bytes accessed | tf_op | source)
XLA Modules:
  0.0 247.0 jit_solution(3087709217008129473)
XLA Ops:
  16.9 6.4 %all-to-all-start = ((bf16[8,1,2]{2,1,0:T(2,128)(2,1)}), bf16[8,1,2]{2,1,0:T(2,128)(2,1)S(1)}, u32[]{:S(2)}, u32[]{:S(2)}) async-start(bf16[8,1,2]{2,1,0:T(2,128)(2,1)} %all_to_all.12), calls=%async_computation | async-start | bytes 8192 | tf_op jit(solution)/shard_map/all_to_all | solution.py:100
  28.8 4.5 %all-to-all-start.1 = ((bf16[8,2,65536]{2,1,0:T(2,128)(2,1)}), bf16[8,2,65536]{2,1,0:T(2,128)(2,1)}, u32[]{:S(2)}, u32[]{:S(2)}) async-start(bf16[8,2,65536]{2,1,0:T(2,128)(2,1)} %reshape.132), calls=%async_computation.1 | async-start | bytes 4194304 | tf_op jit(solution)/shard_map/all_to_all | solution.py:99
  37.3 44.9 %all-to-all-done.1 = bf16[8,2,65536]{2,1,0:T(2,128)(2,1)} async-done(((bf16[8,2,65536]{2,1,0:T(2,128)(2,1)}), bf16[8,2,65536]{2,1,0:T(2,128)(2,1)}, u32[]{:S(2)}, u32[]{:S(2)}) %all-to-all-start.1) | async-done | bytes 2097184 | tf_op jit(solution)/shard_map/all_to_all | solution.py:99
  87.2 26.9 %all-gather.2.cloned.1.call-done = bf16[4,9,128,1024]{3,2,1,0:T(8,128)(2,1)} async-done(((bf16[1,9,128,1024]{3,2,1,0:T(8,128)(2,1)}), bf16[4,9,128,1024]{3,2,1,0:T(8,128)(2,1)}) %all-gather.2.cloned.1.call-update) | async-done | bytes 9437200 | tf_op jit(solution)/shard_map/all_gather | solution.py:11
  114.1 9.2 %copy.106 = bf16[4,9,128,1024]{3,2,0,1:T(8,128)(2,1)} copy(bf16[4,9,128,1024]{3,2,1,0:T(8,128)(2,1)} %all-gather.2.cloned.1.call-done) | data formatting | bytes 18874368 | tf_op jit(solution)/shard_map/all_gather | solution.py:11
  123.3 96.9 %while.11 = (s32[]{:T(128)}, f32[512,1024]{1,0:T(8,128)}, bf16[9,21]{1,0:T(8,128)(2,1)S(1)}, bf16[9,512,1024]{2,1,0:T(8,128)(2,1)}, s32[3]{0:T(128)S(1)}, /*index=5*/s32[]{:T(128)}, s32[]{:T(128)}) while((s32[]{:T(128)}, f32[512,1024]{1,0:T(8,128)}, bf16[9,21]{1,0:T(8,128)(2,1)S(1)}, bf16[9,512,1024]{2,1,0:T(8,128)(2,1)}, ...), condition=%wide.region_2.3_spmd.clone, body=%wide.region_1.2_spmd.clone.sunk | while | flops 422297600 | bytes 33489512 | solution.py:145
  123.9 4.0 %fusion.117 = bf16[1,3,128,128]{3,0,2,1:T(2,128)(2,1)S(1)} fusion(f32[3,21,128,128]{3,2,1,0:T(8,128)S(1)} %fusion.116, bf16[9,21]{1,0:T(8,128)(2,1)S(1)} %get-tuple-element.132, s32[]{:T(128)} %get-tuple-element.123), kind=kOutput, calls=%fused_computation.1.clone.1 | convolution fusion | flops 12386304 | bytes 4227588 | tf_op jit(solution)/shard_map/while/body/eval_jaxpr/cl,dlij->cdij/dot_general | solution.py:28
  133.3 4.0 %fusion.117 = bf16[1,3,128,128]{3,0,2,1:T(2,128)(2,1)S(1)} fusion(f32[3,21,128,128]{3,2,1,0:T(8,128)S(1)} %fusion.116, bf16[9,21]{1,0:T(8,128)(2,1)S(1)} %get-tuple-element.132, s32[]{:T(128)} %get-tuple-element.123), kind=kOutput, calls=%fused_computation.1.clone.1 | convolution fusion | flops 12386304 | bytes 4227588 | tf_op jit(solution)/shard_map/while/body/eval_jaxpr/cl,dlij->cdij/dot_general | solution.py:28
  140.1 3.5 %bitcast_add_fusion.4 = f32[512,1024]{1,0:T(8,128)} fusion(f32[128,4,1024]{2,0,1:T(8,128)S(1)} %add_add_fusion.2, f32[512,1024]{1,0:T(8,128)} %get-tuple-element.124, pred[]{:T(512)S(6)} %compare.11), kind=kLoop, calls=%fused_computation.5.clone.1 | loop fusion | flops 1048576 | bytes 6291457 | tf_op jit(solution)/shard_map/while/body/eval_jaxpr/add | solution.py:143
  144.2 4.0 %fusion.117 = bf16[1,3,128,128]{3,0,2,1:T(2,128)(2,1)S(1)} fusion(f32[3,21,128,128]{3,2,1,0:T(8,128)S(1)} %fusion.116, bf16[9,21]{1,0:T(8,128)(2,1)S(1)} %get-tuple-element.132, s32[]{:T(128)} %get-tuple-element.123), kind=kOutput, calls=%fused_computation.1.clone.1 | convolution fusion | flops 12386304 | bytes 4227588 | tf_op jit(solution)/shard_map/while/body/eval_jaxpr/cl,dlij->cdij/dot_general | solution.py:28
  151.1 3.5 %bitcast_add_fusion.4 = f32[512,1024]{1,0:T(8,128)} fusion(f32[128,4,1024]{2,0,1:T(8,128)S(1)} %add_add_fusion.2, f32[512,1024]{1,0:T(8,128)} %get-tuple-element.124, pred[]{:T(512)S(6)} %compare.11), kind=kLoop, calls=%fused_computation.5.clone.1 | loop fusion | flops 1048576 | bytes 6291457 | tf_op jit(solution)/shard_map/while/body/eval_jaxpr/add | solution.py:143
  155.2 4.0 %fusion.117 = bf16[1,3,128,128]{3,0,2,1:T(2,128)(2,1)S(1)} fusion(f32[3,21,128,128]{3,2,1,0:T(8,128)S(1)} %fusion.116, bf16[9,21]{1,0:T(8,128)(2,1)S(1)} %get-tuple-element.132, s32[]{:T(128)} %get-tuple-element.123), kind=kOutput, calls=%fused_computation.1.clone.1 | convolution fusion | flops 12386304 | bytes 4227588 | tf_op jit(solution)/shard_map/while/body/eval_jaxpr/cl,dlij->cdij/dot_general | solution.py:28
  162.0 3.5 %bitcast_add_fusion.4 = f32[512,1024]{1,0:T(8,128)} fusion(f32[128,4,1024]{2,0,1:T(8,128)S(1)} %add_add_fusion.2, f32[512,1024]{1,0:T(8,128)} %get-tuple-element.124, pred[]{:T(512)S(6)} %compare.11), kind=kLoop, calls=%fused_computation.5.clone.1 | loop fusion | flops 1048576 | bytes 6291457 | tf_op jit(solution)/shard_map/while/body/eval_jaxpr/add | solution.py:143
  166.1 4.0 %fusion.117 = bf16[1,3,128,128]{3,0,2,1:T(2,128)(2,1)S(1)} fusion(f32[3,21,128,128]{3,2,1,0:T(8,128)S(1)} %fusion.116, bf16[9,21]{1,0:T(8,128)(2,1)S(1)} %get-tuple-element.132, s32[]{:T(128)} %get-tuple-element.123), kind=kOutput, calls=%fused_computation.1.clone.1 | convolution fusion | flops 12386304 | bytes 4227588 | tf_op jit(solution)/shard_map/while/body/eval_jaxpr/cl,dlij->cdij/dot_general | solution.py:28
  173.0 3.5 %bitcast_add_fusion.4 = f32[512,1024]{1,0:T(8,128)} fusion(f32[128,4,1024]{2,0,1:T(8,128)S(1)} %add_add_fusion.2, f32[512,1024]{1,0:T(8,128)} %get-tuple-element.124, pred[]{:T(512)S(6)} %compare.11), kind=kLoop, calls=%fused_computation.5.clone.1 | loop fusion | flops 1048576 | bytes 6291457 | tf_op jit(solution)/shard_map/while/body/eval_jaxpr/add | solution.py:143
  177.1 4.0 %fusion.117 = bf16[1,3,128,128]{3,0,2,1:T(2,128)(2,1)S(1)} fusion(f32[3,21,128,128]{3,2,1,0:T(8,128)S(1)} %fusion.116, bf16[9,21]{1,0:T(8,128)(2,1)S(1)} %get-tuple-element.132, s32[]{:T(128)} %get-tuple-element.123), kind=kOutput, calls=%fused_computation.1.clone.1 | convolution fusion | flops 12386304 | bytes 4227588 | tf_op jit(solution)/shard_map/while/body/eval_jaxpr/cl,dlij->cdij/dot_general | solution.py:28
  183.9 3.5 %bitcast_add_fusion.4 = f32[512,1024]{1,0:T(8,128)} fusion(f32[128,4,1024]{2,0,1:T(8,128)S(1)} %add_add_fusion.2, f32[512,1024]{1,0:T(8,128)} %get-tuple-element.124, pred[]{:T(512)S(6)} %compare.11), kind=kLoop, calls=%fused_computation.5.clone.1 | loop fusion | flops 1048576 | bytes 6291457 | tf_op jit(solution)/shard_map/while/body/eval_jaxpr/add | solution.py:143
  188.0 4.0 %fusion.117 = bf16[1,3,128,128]{3,0,2,1:T(2,128)(2,1)S(1)} fusion(f32[3,21,128,128]{3,2,1,0:T(8,128)S(1)} %fusion.116, bf16[9,21]{1,0:T(8,128)(2,1)S(1)} %get-tuple-element.132, s32[]{:T(128)} %get-tuple-element.123), kind=kOutput, calls=%fused_computation.1.clone.1 | convolution fusion | flops 12386304 | bytes 4227588 | tf_op jit(solution)/shard_map/while/body/eval_jaxpr/cl,dlij->cdij/dot_general | solution.py:28
  194.9 3.5 %bitcast_add_fusion.4 = f32[512,1024]{1,0:T(8,128)} fusion(f32[128,4,1024]{2,0,1:T(8,128)S(1)} %add_add_fusion.2, f32[512,1024]{1,0:T(8,128)} %get-tuple-element.124, pred[]{:T(512)S(6)} %compare.11), kind=kLoop, calls=%fused_computation.5.clone.1 | loop fusion | flops 1048576 | bytes 6291457 | tf_op jit(solution)/shard_map/while/body/eval_jaxpr/add | solution.py:143
  198.9 4.0 %fusion.117 = bf16[1,3,128,128]{3,0,2,1:T(2,128)(2,1)S(1)} fusion(f32[3,21,128,128]{3,2,1,0:T(8,128)S(1)} %fusion.116, bf16[9,21]{1,0:T(8,128)(2,1)S(1)} %get-tuple-element.132, s32[]{:T(128)} %get-tuple-element.123), kind=kOutput, calls=%fused_computation.1.clone.1 | convolution fusion | flops 12386304 | bytes 4227588 | tf_op jit(solution)/shard_map/while/body/eval_jaxpr/cl,dlij->cdij/dot_general | solution.py:28
  205.8 3.5 %bitcast_add_fusion.4 = f32[512,1024]{1,0:T(8,128)} fusion(f32[128,4,1024]{2,0,1:T(8,128)S(1)} %add_add_fusion.2, f32[512,1024]{1,0:T(8,128)} %get-tuple-element.124, pred[]{:T(512)S(6)} %compare.11), kind=kLoop, calls=%fused_computation.5.clone.1 | loop fusion | flops 1048576 | bytes 6291457 | tf_op jit(solution)/shard_map/while/body/eval_jaxpr/add | solution.py:143
  209.9 4.0 %fusion.117 = bf16[1,3,128,128]{3,0,2,1:T(2,128)(2,1)S(1)} fusion(f32[3,21,128,128]{3,2,1,0:T(8,128)S(1)} %fusion.116, bf16[9,21]{1,0:T(8,128)(2,1)S(1)} %get-tuple-element.132, s32[]{:T(128)} %get-tuple-element.123), kind=kOutput, calls=%fused_computation.1.clone.1 | convolution fusion | flops 12386304 | bytes 4227588 | tf_op jit(solution)/shard_map/while/body/eval_jaxpr/cl,dlij->cdij/dot_general | solution.py:28
  216.7 3.5 %bitcast_add_fusion.4 = f32[512,1024]{1,0:T(8,128)} fusion(f32[128,4,1024]{2,0,1:T(8,128)S(1)} %add_add_fusion.2, f32[512,1024]{1,0:T(8,128)} %get-tuple-element.124, pred[]{:T(512)S(6)} %compare.11), kind=kLoop, calls=%fused_computation.5.clone.1 | loop fusion | flops 1048576 | bytes 6291457 | tf_op jit(solution)/shard_map/while/body/eval_jaxpr/add | solution.py:143
  220.2 3.0 %copy.108 = f32[512,1024]{0,1:T(8,128)} copy(f32[512,1024]{1,0:T(8,128)} %get-tuple-element.32) | data formatting | bytes 4194304 | tf_op jit(solution)/shard_map/while | solution.py:145
  (148 shorter events, 73.5 us)
Async XLA Ops:
  6.5 0.7 copy-start
  6.5 107.6 %all-gather.2.cloned.1.call-start = ((), (), s32[]{:S(2)}) async-start(), calls=%async_computation.2 | async-start | bytes 11796480 | tf_op jit(solution)/shard_map/all_gather | solution.py:11
  8.6 1.0 copy-start.5
  15.0 0.8 copy-start.8
  15.0 1.0 copy-start.9
  15.0 8.2 %copy-start.4 = (bf16[1,1,16,256,256]{4,3,2,1,0:T(8,128)(2,1)S(1)}, bf16[1,1,16,256,256]{4,3,2,1,0:T(8,128)(2,1)}, u32[]{:S(2)}) copy-start(bf16[1,1,16,256,256]{4,3,2,1,0:T(8,128)(2,1)} %param.12) | copy-start | bytes 6291460
  16.9 11.9 %all-to-all-start = ((bf16[8,1,2]{2,1,0:T(2,128)(2,1)}), bf16[8,1,2]{2,1,0:T(2,128)(2,1)S(1)}, u32[]{:S(2)}, u32[]{:S(2)}) async-start(bf16[8,1,2]{2,1,0:T(2,128)(2,1)} %all_to_all.12), calls=%async_computation | async-start | bytes 8192 | tf_op jit(solution)/shard_map/all_to_all | solution.py:100
  27.5 5.9 %copy-start.10 = (bf16[1,2,25]{2,1,0:T(2,128)(2,1)S(1)}, bf16[1,2,25]{2,1,0:T(2,128)(2,1)}, u32[]{:S(2)}) copy-start(bf16[1,2,25]{2,1,0:T(2,128)(2,1)} %param.21) | copy-start | bytes 304
  28.8 53.4 %all-to-all-start.1 = ((bf16[8,2,65536]{2,1,0:T(2,128)(2,1)}), bf16[8,2,65536]{2,1,0:T(2,128)(2,1)}, u32[]{:S(2)}, u32[]{:S(2)}) async-start(bf16[8,2,65536]{2,1,0:T(2,128)(2,1)} %reshape.132), calls=%async_computation.1 | async-start | bytes 4194304 | tf_op jit(solution)/shard_map/all_to_all | solution.py:99
  33.4 2.1 copy-start.6
  33.4 2.1 copy-start.7
  33.4 2.1 copy-start.11
  220.2 3.0 %copy-start.2 = (f32[512,1024]{0,1:T(8,128)S(1)}, f32[512,1024]{0,1:T(8,128)}, u32[]{:S(2)}) copy-start(f32[512,1024]{0,1:T(8,128)} %copy.107) | copy-start | bytes 6291460
  230.0 1.2 copy-start.3
  238.2 1.9 copy-start.1
Sparse Core Ops, SparseCore 0:
  15.2 98.9 all-gather.1
